TPU v7x, 128 devices: a whole 4x4x4 slice. The times are simulated.
128 devices in a mesh: prow: 8 (over y, core), pcol: 16 (over x, z).
Axes of the slice: x: 4, y: 4, z: 4, core: 2. Of those that a mesh axis runs over, the one named last changes fastest.
Arguments:
- right_sides: bfloat16 [32768, 128], P(('prow', 'pcol')), may hold values from -6 to 6
- factor: bfloat16 [16, 16, 32, 8, 128, 128], P(None, 'pcol', None, 'prow'), may hold values from -0.046875 to 0.046875
- pattern: int32 [16, 16, 32, 8], P(None, 'pcol', None, 'prow'), may hold values 0 or 1
- lower_inverse: bfloat16 [16, 16, 128, 128], P(None, 'pcol'), may hold values from -0.5 to 0.5
- upper_inverse: bfloat16 [16, 16, 128, 128], P(None, 'pcol'), may hold values from -0.5 to 0.5
Outputs:
- solution: bfloat16 [32768, 128], P(('prow', 'pcol'))
All inputs are finite; a program needn't handle non-finite values. No bound on the sum of `pattern` on one device may be relied on, other than what follows from the above.
Results may differ from a plain program's by a relative error of at most 0.02.
Values may be sent and summed in bfloat16 or wider, within the bound.
A program may use at most 128 MiB of HBM per device.

v0:
```python
import jax
import jax.numpy as jnp
from jax import lax
from jax.sharding import PartitionSpec as P


def level_index(index_vals, node_count):
    bounds = (node_count // 2, 3 * node_count // 4, 7 * node_count // 8)
    result = jnp.zeros(index_vals.shape, jnp.int32)
    for edge_val in bounds:
        result = result + (index_vals >= edge_val).astype(jnp.int32)
    return result


def level_sums(
    blocks,
    pattern_loc,
    col_levels,
    solved_all,
    row_id,
    prow_n,
    row_start,
    row_end,
    col_start,
    col_end,
    level_id,
    upward,
):
    if col_end <= col_start:
        return None
    block_size = blocks.shape[2]
    rhs_count = solved_all.shape[2]
    grouped = solved_all.reshape(-1, prow_n, block_size, rhs_count)
    column_vals = lax.dynamic_index_in_dim(grouped, row_id, 1, keepdims=False)[col_start:col_end]
    levels_here = col_levels[col_start:col_end]
    if upward:
        order_mask = levels_here > level_id
    else:
        order_mask = levels_here < level_id
    keep_mask = (pattern_loc[row_start:row_end, col_start:col_end] > 0) & order_mask[None, :]
    masked = jnp.where(
        keep_mask[:, :, None, None],
        blocks[row_start:row_end, col_start:col_end],
        jnp.zeros((), jnp.bfloat16),
    )
    return jnp.einsum("ijab,jbn->ian", masked, column_vals, preferred_element_type=jnp.float32)


def finish_level(partial_value, base_rows, inverse_rows, pcol_n):
    row_count = base_rows.shape[0]
    block_size = base_rows.shape[1]
    rhs_count = base_rows.shape[2]
    if partial_value is None:
        remainder = base_rows
    else:
        summed = lax.psum(partial_value.astype(jnp.bfloat16), "prow").astype(jnp.float32)
        remainder = (base_rows.astype(jnp.float32) - summed).astype(jnp.bfloat16)
    solved = jnp.einsum(
        "iab,ibn->ian", inverse_rows, remainder, preferred_element_type=jnp.float32
    ).astype(jnp.bfloat16)
    gathered = lax.all_gather(solved[:, None], "pcol", axis=1, tiled=True)
    return gathered.reshape(row_count * pcol_n, block_size, rhs_count)


def on_device(right_sides, factor, pattern, lower_inverse, upper_inverse):
    prow_n = lax.axis_size("prow")
    pcol_n = lax.axis_size("pcol")
    row_id = lax.axis_index("prow")
    col_id = lax.axis_index("pcol")
    blocks = factor[:, 0, :, 0]
    pattern_loc = pattern[:, 0, :, 0]
    lower_rows = lower_inverse[:, 0]
    upper_rows = upper_inverse[:, 0]
    row_blocks = blocks.shape[0]
    col_blocks = blocks.shape[1]
    block_size = blocks.shape[2]
    rhs_count = right_sides.shape[1]
    node_count = row_blocks * pcol_n
    everything = lax.all_gather(right_sides, ("prow", "pcol"), axis=0, tiled=True)
    everything = everything.reshape(row_blocks, pcol_n, block_size, rhs_count)
    mine_right = lax.dynamic_index_in_dim(everything, col_id, 1, keepdims=False)
    col_levels = level_index(jnp.arange(col_blocks, dtype=jnp.int32) * prow_n + row_id, node_count)
    bounds = (0, row_blocks // 2, 3 * row_blocks // 4, 7 * row_blocks // 8, row_blocks)
    forward_vals = jnp.zeros((node_count, block_size, rhs_count), jnp.bfloat16)
    for level_id in range(4):
        row_start, row_end = (bounds[level_id], bounds[level_id + 1])
        col_end = min(col_blocks, -(-(row_start * pcol_n) // prow_n))
        partial_value = level_sums(
            blocks,
            pattern_loc,
            col_levels,
            forward_vals,
            row_id,
            prow_n,
            row_start,
            row_end,
            0,
            col_end,
            level_id,
            False,
        )
        solved = finish_level(
            partial_value, mine_right[row_start:row_end], lower_rows[row_start:row_end], pcol_n
        )
        forward_vals = lax.dynamic_update_slice_in_dim(forward_vals, solved, row_start * pcol_n, 0)
    forward_mine = lax.dynamic_index_in_dim(
        forward_vals.reshape(row_blocks, pcol_n, block_size, rhs_count), col_id, 1, keepdims=False
    )
    backward_vals = jnp.zeros((node_count, block_size, rhs_count), jnp.bfloat16)
    for level_id in (3, 2, 1, 0):
        row_start, row_end = (bounds[level_id], bounds[level_id + 1])
        col_start = row_end * pcol_n // prow_n
        partial_value = level_sums(
            blocks,
            pattern_loc,
            col_levels,
            backward_vals,
            row_id,
            prow_n,
            row_start,
            row_end,
            col_start,
            col_blocks,
            level_id,
            True,
        )
        solved = finish_level(
            partial_value, forward_mine[row_start:row_end], upper_rows[row_start:row_end], pcol_n
        )
        backward_vals = lax.dynamic_update_slice_in_dim(
            backward_vals, solved, row_start * pcol_n, 0
        )
    out_rows = right_sides.shape[0]
    device_id = row_id * pcol_n + col_id
    flat = backward_vals.reshape(node_count * block_size, rhs_count)
    return lax.dynamic_slice_in_dim(flat, device_id * out_rows, out_rows, 0)


def solution(mesh):
    placed = (
        P(("prow", "pcol"), None),
        P(None, "pcol", None, "prow", None, None),
        P(None, "pcol", None, "prow"),
        P(None, "pcol", None, None),
        P(None, "pcol", None, None),
    )
    return jax.shard_map(
        on_device, mesh=mesh, in_specs=placed, out_specs=P(("prow", "pcol"), None), check_vma=False
    )
```

profile of v0, /device:TPU:0, one launch (start us, length us, event | category | flops | bytes accessed | tf_op | source)
XLA Modules:
  0.0 902.8 jit_solution(18157509265006647587)
XLA Ops:
  6.5 0.7 all-gather.18.cloned.1.call-update
  7.3 75.4 %all-gather.18.cloned.1.call-done = bf16[32768,128]{1,0:T(8,128)(2,1)} async-done(((bf16[256,128]{1,0:T(8,128)(2,1)}), bf16[32768,128]{1,0:T(8,128)(2,1)}) %all-gather.18.cloned.1.call-update) | async-done | bytes 8388624 | tf_op jit(solution)/shard_map/all_gather | solution.py:79
  82.7 2.1 fusion.11
  84.9 0.1 slice_compare_fusion.3
  85.0 0.7 fusion.61
  85.7 53.7 %all-gather.20.cloned.1.call-done = bf16[8,2048,128]{1,2,0:T(8,128)(2,1)} async-done(((bf16[8,128,128]{1,2,0:T(8,128)(2,1)}), bf16[8,2048,128]{1,2,0:T(8,128)(2,1)}) %all-gather.20.cloned.1.call-update) | async-done | bytes 4194320 | tf_op jit(solution)/shard_map/all_gather | solution.py:61
  139.4 6.5 copy.16
  145.9 4.1 dynamic_update_slice.24
  150.0 3.2 copy-done
  153.2 3.1 fusion.15
  156.4 0.9 constant_dynamic-slice_fusion.3
  157.4 0.1 copy.40
  157.5 58.3 %all-reduce.9.cloned.1.call-done = bf16[4,128,128]{1,2,0:T(8,128)(2,1)} async-done(((bf16[4,128,128]{1,2,0:T(8,128)(2,1)}), bf16[4,128,128]{1,2,0:T(8,128)(2,1)}) %all-reduce.9.cloned.1.call-update) | async-done | bytes 131088 | tf_op jit(solution)/shard_map/psum | solution.py:56
  215.8 1.8 fusion.17
  217.7 46.2 %all-gather.22.cloned.1.call-done = bf16[4,2048,128]{1,2,0:T(8,128)(2,1)} async-done(((bf16[4,128,128]{1,2,0:T(8,128)(2,1)}), bf16[4,2048,128]{1,2,0:T(8,128)(2,1)}) %all-gather.22.cloned.1.call-update) | async-done | bytes 2097168 | tf_op jit(solution)/shard_map/all_gather | solution.py:61
  263.9 3.0 copy.18
  267.0 1.4 constant_dynamic-update-slice_fusion.5
  268.4 3.0 fusion.22
  271.5 0.9 constant_dynamic-slice_fusion.6
  272.4 0.1 copy.41
  272.6 58.2 %all-reduce.11.cloned.1.call-done = bf16[2,128,128]{1,2,0:T(8,128)(2,1)} async-done(((bf16[2,128,128]{1,2,0:T(8,128)(2,1)}), bf16[2,128,128]{1,2,0:T(8,128)(2,1)}) %all-reduce.11.cloned.1.call-update) | async-done | bytes 65552 | tf_op jit(solution)/shard_map/psum | solution.py:56
  330.8 1.6 fusion.23
  332.5 42.4 %all-gather.24.cloned.1.call-done = bf16[2,2048,128]{1,2,0:T(8,128)(2,1)} async-done(((bf16[2,128,128]{1,2,0:T(8,128)(2,1)}), bf16[2,2048,128]{1,2,0:T(8,128)(2,1)}) %all-gather.24.cloned.1.call-update) | async-done | bytes 1048592 | tf_op jit(solution)/shard_map/all_gather | solution.py:61
  374.9 1.6 copy.20
  376.5 1.1 constant_dynamic-update-slice_fusion.4
  377.6 3.2 fusion.20
  380.8 0.1 copy.42
  381.0 59.0 %all-reduce.13.cloned.1.call-done = bf16[2,128,128]{1,2,0:T(8,128)(2,1)} async-done(((bf16[2,128,128]{1,2,0:T(8,128)(2,1)}), bf16[2,128,128]{1,2,0:T(8,128)(2,1)}) %all-reduce.13.cloned.1.call-update) | async-done | bytes 65552 | tf_op jit(solution)/shard_map/psum | solution.py:56
  440.0 1.6 fusion.24
  441.7 42.6 %all-gather.26.cloned.1.call-done = bf16[2,2048,128]{1,2,0:T(8,128)(2,1)} async-done(((bf16[2,128,128]{1,2,0:T(8,128)(2,1)}), bf16[2,2048,128]{1,2,0:T(8,128)(2,1)}) %all-gather.26.cloned.1.call-update) | async-done | bytes 1048592 | tf_op jit(solution)/shard_map/all_gather | solution.py:61
  484.3 1.6 copy.22
  485.9 1.1 constant_dynamic-update-slice_fusion.3
  487.0 1.7 fusion.25
  488.8 0.1 compare_and_fusion
  488.9 42.5 %all-gather.28.cloned.1.call-done = bf16[2,2048,128]{1,2,0:T(8,128)(2,1)} async-done(((bf16[2,128,128]{1,2,0:T(8,128)(2,1)}), bf16[2,2048,128]{1,2,0:T(8,128)(2,1)}) %all-gather.28.cloned.1.call-update) | async-done | bytes 1048592 | tf_op jit(solution)/shard_map/all_gather | solution.py:61
  531.3 1.6 copy.25
  533.0 5.3 dynamic_update_slice.28
  538.3 1.9 fusion.21
  540.3 0.9 constant_dynamic-slice_fusion.1
  541.1 0.1 copy.45
  541.3 58.2 %all-reduce.15.cloned.1.call-done = bf16[2,128,128]{1,2,0:T(8,128)(2,1)} async-done(((bf16[2,128,128]{1,2,0:T(8,128)(2,1)}), bf16[2,128,128]{1,2,0:T(8,128)(2,1)}) %all-reduce.15.cloned.1.call-update) | async-done | bytes 65552 | tf_op jit(solution)/shard_map/psum | solution.py:56
  599.4 1.6 fusion.26
  601.2 0.1 fusion.62
  601.3 42.4 %all-gather.30.cloned.1.call-done = bf16[2,2048,128]{1,2,0:T(8,128)(2,1)} async-done(((bf16[2,128,128]{1,2,0:T(8,128)(2,1)}), bf16[2,2048,128]{1,2,0:T(8,128)(2,1)}) %all-gather.30.cloned.1.call-update) | async-done | bytes 1048592 | tf_op jit(solution)/shard_map/all_gather | solution.py:61
  643.7 1.6 copy.27
  645.3 1.0 constant_dynamic-update-slice_fusion.2
  646.4 2.5 fusion.14
  648.9 0.9 constant_dynamic-slice_fusion
  649.8 0.1 copy.46
  650.0 58.2 %all-reduce.17.cloned.1.call-done = bf16[4,128,128]{1,2,0:T(8,128)(2,1)} async-done(((bf16[4,128,128]{1,2,0:T(8,128)(2,1)}), bf16[4,128,128]{1,2,0:T(8,128)(2,1)}) %all-reduce.17.cloned.1.call-update) | async-done | bytes 131088 | tf_op jit(solution)/shard_map/psum | solution.py:56
  708.2 1.8 fusion.18
  710.0 0.1 fusion.60
  710.1 46.3 %all-gather.32.cloned.1.call-done = bf16[4,2048,128]{1,2,0:T(8,128)(2,1)} async-done(((bf16[4,128,128]{1,2,0:T(8,128)(2,1)}), bf16[4,2048,128]{1,2,0:T(8,128)(2,1)}) %all-gather.32.cloned.1.call-update) | async-done | bytes 2097168 | tf_op jit(solution)/shard_map/all_gather | solution.py:61
  756.5 3.0 copy.29
  759.5 1.5 constant_dynamic-update-slice_fusion.1
  761.0 4.6 fusion.10
  765.6 1.0 constant_dynamic-slice_fusion.5
  766.6 0.2 copy.47
  766.8 58.6 %all-reduce.19.cloned.1.call-done = bf16[8,128,128]{1,2,0:T(8,128)(2,1)} async-done(((bf16[8,128,128]{1,2,0:T(8,128)(2,1)}), bf16[8,128,128]{1,2,0:T(8,128)(2,1)}) %all-reduce.19.cloned.1.call-update) | async-done | bytes 262160 | tf_op jit(solution)/shard_map/psum | solution.py:56
  825.4 2.0 fusion.12
  827.4 56.1 %all-gather.34.cloned.1.call-done = bf16[8,2048,128]{1,2,0:T(8,128)(2,1)} async-done(((bf16[8,128,128]{1,2,0:T(8,128)(2,1)}), bf16[8,2048,128]{1,2,0:T(8,128)(2,1)}) %all-gather.34.cloned.1.call-update) | async-done | bytes 4194320 | tf_op jit(solution)/shard_map/all_gather | solution.py:61
  883.5 6.5 copy.31
  890.0 4.7 constant_dynamic-update-slice_fusion
  894.8 1.5 constant_dynamic-slice_fusion.4
  (43 shorter events, 1.0 us)
Async XLA Ops:
  6.5 76.2 %all-gather.18.cloned.1.call-start = ((), (), s32[]{:S(2)}) async-start(), calls=%async_computation | async-start | bytes 8454144 | tf_op jit(solution)/shard_map/all_gather | solution.py:79
  7.3 132.1 %all-gather.20.cloned.1.call-start = ((), (), s32[]{:S(2)}) async-start(), calls=%async_computation.7 | async-start | bytes 4456448 | tf_op jit(solution)/shard_map/all_gather | solution.py:61
  84.8 131.0 %all-reduce.9.cloned.1.call-start = ((), (), s32[]{:S(2)}) async-start(), calls=%async_computation.1 | async-start | bytes 262144 | tf_op jit(solution)/shard_map/psum | solution.py:56
  145.9 69.9 %copy-start.1 = (bf16[16,1,128,128]{3,2,1,0:T(8,128)(2,1)S(1)}, bf16[16,1,128,128]{3,2,1,0:T(8,128)(2,1)}, u32[]{:S(2)}) copy-start(bf16[16,1,128,128]{3,2,1,0:T(8,128)(2,1)} %param.8) | copy-start | bytes 1572868
  145.9 71.8 %copy-start.3 = (s32[16,1,32,1]{2,3,1,0:T(1,128)S(1)}, s32[16,1,32,1]{2,3,1,0:T(1,128)}, u32[]{:S(2)}) copy-start(s32[16,1,32,1]{2,3,1,0:T(1,128)} %param.7) | copy-start | bytes 6148
  150.0 3.2 copy-start
  156.4 107.5 %all-gather.22.cloned.1.call-start = ((), (), s32[]{:S(2)}) async-start(), calls=%async_computation.8 | async-start | bytes 2228224 | tf_op jit(solution)/shard_map/all_gather | solution.py:61
  217.6 113.2 %all-reduce.11.cloned.1.call-start = ((), (), s32[]{:S(2)}) async-start(), calls=%async_computation.2 | async-start | bytes 131072 | tf_op jit(solution)/shard_map/psum | solution.py:56
  268.4 218.5 %copy-start.2 = (bf16[16,1,128,128]{3,2,1,0:T(8,128)(2,1)S(1)}, bf16[16,1,128,128]{3,2,1,0:T(8,128)(2,1)}, u32[]{:S(2)}) copy-start(bf16[16,1,128,128]{3,2,1,0:T(8,128)(2,1)} %param.9) | copy-start | bytes 1572868
  271.5 103.4 %all-gather.24.cloned.1.call-start = ((), (), s32[]{:S(2)}) async-start(), calls=%async_computation.9 | async-start | bytes 1114112 | tf_op jit(solution)/shard_map/all_gather | solution.py:61
  332.4 107.6 %all-reduce.13.cloned.1.call-start = ((), (), s32[]{:S(2)}) async-start(), calls=%async_computation.3 | async-start | bytes 131072 | tf_op jit(solution)/shard_map/psum | solution.py:56
  380.8 103.5 %all-gather.26.cloned.1.call-start = ((), (), s32[]{:S(2)}) async-start(), calls=%async_computation.10 | async-start | bytes 1114112 | tf_op jit(solution)/shard_map/all_gather | solution.py:61
  441.7 89.7 %all-gather.28.cloned.1.call-start = ((), (), s32[]{:S(2)}) async-start(), calls=%async_computation.11 | async-start | bytes 1114112 | tf_op jit(solution)/shard_map/all_gather | solution.py:61
  488.7 110.8 %all-reduce.15.cloned.1.call-start = ((), (), s32[]{:S(2)}) async-start(), calls=%async_computation.4 | async-start | bytes 131072 | tf_op jit(solution)/shard_map/psum | solution.py:56
  540.2 103.5 %all-gather.30.cloned.1.call-start = ((), (), s32[]{:S(2)}) async-start(), calls=%async_computation.12 | async-start | bytes 1114112 | tf_op jit(solution)/shard_map/all_gather | solution.py:61
  601.1 107.1 %all-reduce.17.cloned.1.call-start = ((), (), s32[]{:S(2)}) async-start(), calls=%async_computation.5 | async-start | bytes 262144 | tf_op jit(solution)/shard_map/psum | solution.py:56
  648.9 107.6 %all-gather.32.cloned.1.call-start = ((), (), s32[]{:S(2)}) async-start(), calls=%async_computation.13 | async-start | bytes 2228224 | tf_op jit(solution)/shard_map/all_gather | solution.py:61
  710.0 115.4 %all-reduce.19.cloned.1.call-start = ((), (), s32[]{:S(2)}) async-start(), calls=%async_computation.6 | async-start | bytes 524288 | tf_op jit(solution)/shard_map/psum | solution.py:56
  765.6 117.9 %all-gather.34.cloned.1.call-start = ((), (), s32[]{:S(2)}) async-start(), calls=%async_computation.14 | async-start | bytes 4456448 | tf_op jit(solution)/shard_map/all_gather | solution.py:61
Sparse Core Ops, SparseCore 0:
  10.5 72.1 all-gather.17
  84.9 54.4 all-gather.19
  156.5 59.2 all-reduce.8
  217.8 46.0 all-gather.21
  271.6 59.1 all-reduce.10
  332.7 42.1 all-gather.23
  380.9 59.0 all-reduce.12
  442.1 42.1 all-gather.25
  488.8 42.5 all-gather.27
  540.4 59.0 all-reduce.14
  601.6 42.1 all-gather.29
  649.0 59.1 all-reduce.16
  710.3 46.0 all-gather.31
  765.7 59.6 all-reduce.18
  827.5 55.9 all-gather.33
where the time goes:
time: 904 us; the launch traced here: 903 us
  waiting for transfers between devices  799 us (88%)
  local copies, waits for them, and re-layouts  55.9 us (6%)
  matrix products  32.5 us (4%)
  between operations  13.5 us (1%)
    all_gather x8, waiting for transfers between devices, finish_level(): gathered = lax.all_gather(solved[:, None], 'pcol', axis=1, tiled=True)  372 us
    psum x6, waiting for transfers between devices, finish_level(): lax.psum(partial_value.astype(jnp.bfloat16), 'prow').astype(jnp.float32)  351 us
    all_gather x1, waiting for transfers between devices, on_device(): lax.all_gather(right_sides, ('prow', 'pcol'), axis=0, tiled=True)  75.4 us
    all_gather x8, local copies, waits for them, and re-layouts, finish_level(): gathered = lax.all_gather(solved[:, None], 'pcol', axis=1, tiled=True)  25.4 us
    dot_general x6, matrix products, level_sums(): jnp.einsum('ijab,jbn->ian', masked, column_vals, preferred_element_type=j...  18.3 us
  transfers between devices with their start and end apart: 15, of which 15 were waited for; matrix products, arithmetic and copies ran while one was open for 1% of the time, Pallas kernels for 0%

commit v1 on v0

--- a/solution.py
+++ b/solution.py
@@ -53,7 +53,9 @@
     if partial_value is None:
         remainder = base_rows
     else:
-        summed = lax.psum(partial_value.astype(jnp.bfloat16), "prow").astype(jnp.float32)
+        summed = jnp.sum(lax.all_gather(partial_value.astype(jnp.bfloat16), "prow"), axis=0).astype(
+            jnp.float32
+        )
         remainder = (base_rows.astype(jnp.float32) - summed).astype(jnp.bfloat16)
     solved = jnp.einsum(
         "iab,ibn->ian", inverse_rows, remainder, preferred_element_type=jnp.float32

time: 904 us -> 658 us (0.73)
  waiting for transfers between devices: 799 us -> 514 us
  blocking collectives: 0 us -> 40.5 us
    psum x6 -> x0, waiting for transfers between devices: 351 us -> none  [finish_level(): lax.psum(partial_value.astype(jnp.bfloat16), 'prow').astype(jnp.float32)]
    all_gather x0 -> x3, waiting for transfers between devices: none -> 66.6 us  [finish_level(): lax.all_gather(partial_value.astype(jnp.bfloat16), 'prow')]
    all_gather x0 -> x3, blocking collectives: none -> 40.5 us  [finish_level(): lax.all_gather(partial_value.astype(jnp.bfloat16), 'prow')]
  transfers between devices with their start and end apart: 15 -> 12, of which waited for: 15 -> 12; matrix products, arithmetic and copies ran while one was open for 1% -> 1% of each run, Pallas kernels for 0% -> 0%
where the time goes in v1:
time: 658 us; the launch traced here: 657 us
  waiting for transfers between devices  514 us (78%)
  local copies, waits for them, and re-layouts  56.5 us (9%)
  blocking collectives  40.5 us (6%)
  matrix products  24.6 us (4%)
  between operations  13.8 us (2%)
    all_gather x8, waiting for transfers between devices, finish_level(): gathered = lax.all_gather(solved[:, None], 'pcol', axis=1, tiled=True)  371 us
    all_gather x1, waiting for transfers between devices, on_device(): lax.all_gather(right_sides, ('prow', 'pcol'), axis=0, tiled=True)  75.4 us
    all_gather x3, waiting for transfers between devices, finish_level(): lax.all_gather(partial_value.astype(jnp.bfloat16), 'prow')  66.6 us
    all_gather x3, blocking collectives, finish_level(): lax.all_gather(partial_value.astype(jnp.bfloat16), 'prow')  40.5 us
    all_gather x8, local copies, waits for them, and re-layouts, finish_level(): gathered = lax.all_gather(solved[:, None], 'pcol', axis=1, tiled=True)  25.4 us
    dot_general x6, matrix products, level_sums(): jnp.einsum('ijab,jbn->ian', masked, column_vals, preferred_element_type=j...  15.6 us
  transfers between devices with their start and end apart: 12, of which 12 were waited for; matrix products, arithmetic and copies ran while one was open for 1% of the time, Pallas kernels for 0%

profile of v1, /device:TPU:0, one launch (start us, length us, event | category | flops | bytes accessed | tf_op | source)
XLA Modules:
  0.0 656.6 jit_solution(1309259279871560548)
XLA Ops:
  6.5 0.7 all-gather.27.cloned.1.call-update
  7.3 75.4 %all-gather.27.cloned.1.call-done = bf16[32768,128]{1,0:T(8,128)(2,1)} async-done(((bf16[256,128]{1,0:T(8,128)(2,1)}), bf16[32768,128]{1,0:T(8,128)(2,1)}) %all-gather.27.cloned.1.call-update) | async-done | bytes 8388624 | tf_op jit(solution)/shard_map/all_gather | solution.py:81
  82.7 2.1 fusion.11
  85.0 0.7 fusion.61
  85.7 53.7 %all-gather.29.cloned.1.call-done = bf16[8,2048,128]{1,2,0:T(8,128)(2,1)} async-done(((bf16[8,128,128]{1,2,0:T(8,128)(2,1)}), bf16[8,2048,128]{1,2,0:T(8,128)(2,1)}) %all-gather.29.cloned.1.call-update) | async-done | bytes 4194320 | tf_op jit(solution)/shard_map/all_gather | solution.py:63
  139.4 6.4 copy.40
  145.8 4.1 dynamic_update_slice.24
  150.0 3.2 copy-done
  153.2 3.0 fusion.15
  156.3 0.9 constant_dynamic-slice_fusion.3
  157.2 0.1 copy.76
  157.3 21.6 %all-gather.31.cloned.1.call-done = bf16[32,128,128]{2,1,0:T(8,128)(2,1)} async-done(((bf16[4,128,128]{2,1,0:T(8,128)(2,1)}), bf16[32,128,128]{2,1,0:T(8,128)(2,1)}) %all-gather.31.cloned.1.call-update) | async-done | bytes 1048592 | tf_op jit(solution)/shard_map/all_gather | solution.py:56
  178.9 1.4 reduce_sum.72
  180.3 0.1 copy.42
  180.4 0.9 fusion.17
  181.4 0.9 constant_dynamic-slice_fusion.6
  182.4 46.1 %all-gather.33.cloned.1.call-done = bf16[4,2048,128]{1,2,0:T(8,128)(2,1)} async-done(((bf16[4,128,128]{1,2,0:T(8,128)(2,1)}), bf16[4,2048,128]{1,2,0:T(8,128)(2,1)}) %all-gather.33.cloned.1.call-update) | async-done | bytes 2097168 | tf_op jit(solution)/shard_map/all_gather | solution.py:63
  228.6 3.0 copy.44
  231.6 1.5 constant_dynamic-update-slice_fusion.5
  233.1 2.2 fusion.22
  235.3 13.6 %all-gather.3 = bf16[16,128,128]{2,1,0:T(8,128)(2,1)S(1)} all-gather(bf16[2,128,128]{2,1,0:T(8,128)(2,1)S(1)} %fusion.22), channel_id=5, replica_groups=mesh['prow'=8,'pcol'=16] {'prow'}, dimensions={0}, use_global_device_ids=true | all-gather | bytes 589824 | tf_op jit(solution)/shard_map/all_gather | solution.py:56
  249.1 0.8 fusion.23
  250.1 41.9 %all-gather.35.cloned.1.call-done = bf16[2,2048,128]{1,2,0:T(8,128)(2,1)} async-done(((bf16[2,128,128]{1,2,0:T(8,128)(2,1)}), bf16[2,2048,128]{1,2,0:T(8,128)(2,1)}) %all-gather.35.cloned.1.call-update) | async-done | bytes 1048592 | tf_op jit(solution)/shard_map/all_gather | solution.py:63
  292.0 1.6 copy.48
  293.6 1.1 constant_dynamic-update-slice_fusion.4
  294.7 2.4 fusion.20
  297.1 13.4 %all-gather.5 = bf16[16,128,128]{2,1,0:T(8,128)(2,1)S(1)} all-gather(bf16[2,128,128]{2,1,0:T(8,128)(2,1)S(1)} %fusion.20), channel_id=7, replica_groups=mesh['prow'=8,'pcol'=16] {'prow'}, dimensions={0}, use_global_device_ids=true | all-gather | bytes 589824 | tf_op jit(solution)/shard_map/all_gather | solution.py:56
  310.7 0.8 fusion.24
  311.6 42.0 %all-gather.37.cloned.1.call-done = bf16[2,2048,128]{1,2,0:T(8,128)(2,1)} async-done(((bf16[2,128,128]{1,2,0:T(8,128)(2,1)}), bf16[2,2048,128]{1,2,0:T(8,128)(2,1)}) %all-gather.37.cloned.1.call-update) | async-done | bytes 1048592 | tf_op jit(solution)/shard_map/all_gather | solution.py:63
  353.6 1.6 copy.52
  355.2 1.0 constant_dynamic-update-slice_fusion.3
  356.3 1.7 fusion.25
  358.2 0.8 constant_dynamic-slice_fusion.1
  359.2 41.5 %all-gather.39.cloned.1.call-done = bf16[2,2048,128]{1,2,0:T(8,128)(2,1)} async-done(((bf16[2,128,128]{1,2,0:T(8,128)(2,1)}), bf16[2,2048,128]{1,2,0:T(8,128)(2,1)}) %all-gather.39.cloned.1.call-update) | async-done | bytes 1048592 | tf_op jit(solution)/shard_map/all_gather | solution.py:63
  400.7 1.6 copy.55
  402.3 5.3 dynamic_update_slice.28
  407.6 1.2 fusion.21
  408.9 13.4 %all-gather.8 = bf16[16,128,128]{2,1,0:T(8,128)(2,1)S(1)} all-gather(bf16[2,128,128]{2,1,0:T(8,128)(2,1)S(1)} %fusion.21), channel_id=10, replica_groups=mesh['prow'=8,'pcol'=16] {'prow'}, dimensions={0}, use_global_device_ids=true | all-gather | bytes 589824 | tf_op jit(solution)/shard_map/all_gather | solution.py:56
  422.5 0.8 fusion.26
  423.5 41.9 %all-gather.41.cloned.1.call-done = bf16[2,2048,128]{1,2,0:T(8,128)(2,1)} async-done(((bf16[2,128,128]{1,2,0:T(8,128)(2,1)}), bf16[2,2048,128]{1,2,0:T(8,128)(2,1)}) %all-gather.41.cloned.1.call-update) | async-done | bytes 1048592 | tf_op jit(solution)/shard_map/all_gather | solution.py:63
  465.4 1.6 copy.59
  467.0 1.0 constant_dynamic-update-slice_fusion.2
  468.1 2.4 fusion.14
  470.6 0.9 constant_dynamic-slice_fusion
  471.5 0.1 copy.90
  471.6 21.6 %all-gather.43.cloned.1.call-done = bf16[32,128,128]{2,1,0:T(8,128)(2,1)} async-done(((bf16[4,128,128]{2,1,0:T(8,128)(2,1)}), bf16[32,128,128]{2,1,0:T(8,128)(2,1)}) %all-gather.43.cloned.1.call-update) | async-done | bytes 1048592 | tf_op jit(solution)/shard_map/all_gather | solution.py:56
  493.2 1.4 reduce_sum.76
  494.6 0.1 copy.61
  494.7 0.9 fusion.18
  495.6 0.2 all-gather.47.cloned.1.call-start
  495.9 46.9 %all-gather.45.cloned.1.call-done = bf16[4,2048,128]{1,2,0:T(8,128)(2,1)} async-done(((bf16[4,128,128]{1,2,0:T(8,128)(2,1)}), bf16[4,2048,128]{1,2,0:T(8,128)(2,1)}) %all-gather.45.cloned.1.call-update) | async-done | bytes 2097168 | tf_op jit(solution)/shard_map/all_gather | solution.py:63
  542.8 3.0 copy.63
  545.9 1.5 constant_dynamic-update-slice_fusion.1
  547.4 4.3 fusion.10
  551.7 1.0 constant_dynamic-slice_fusion.5
  552.7 0.2 copy.93
  552.9 23.5 %all-gather.47.cloned.1.call-done = bf16[64,128,128]{2,1,0:T(8,128)(2,1)} async-done(((bf16[8,128,128]{2,1,0:T(8,128)(2,1)}), bf16[64,128,128]{2,1,0:T(8,128)(2,1)}) %all-gather.47.cloned.1.call-update) | async-done | bytes 2097168 | tf_op jit(solution)/shard_map/all_gather | solution.py:56
  576.4 2.0 reduce_sum.77
  578.4 0.2 copy.65
  578.6 1.0 fusion.12
  579.6 57.5 %all-gather.49.cloned.1.call-done = bf16[8,2048,128]{1,2,0:T(8,128)(2,1)} async-done(((bf16[8,128,128]{1,2,0:T(8,128)(2,1)}), bf16[8,2048,128]{1,2,0:T(8,128)(2,1)}) %all-gather.49.cloned.1.call-update) | async-done | bytes 4194320 | tf_op jit(solution)/shard_map/all_gather | solution.py:63
  637.1 6.5 copy.67
  643.5 4.7 constant_dynamic-update-slice_fusion
  648.3 1.5 constant_dynamic-slice_fusion.4
  (49 shorter events, 2.0 us)
Async XLA Ops:
  6.5 76.2 %all-gather.27.cloned.1.call-start = ((), (), s32[]{:S(2)}) async-start(), calls=%async_computation | async-start | bytes 8454144 | tf_op jit(solution)/shard_map/all_gather | solution.py:81
  7.3 132.1 %all-gather.29.cloned.1.call-start = ((), (), s32[]{:S(2)}) async-start(), calls=%async_computation.1 | async-start | bytes 4456448 | tf_op jit(solution)/shard_map/all_gather | solution.py:63
  84.8 94.1 %all-gather.31.cloned.1.call-start = ((), (), s32[]{:S(2)}) async-start(), calls=%async_computation.2 | async-start | bytes 1179648 | tf_op jit(solution)/shard_map/all_gather | solution.py:56
  145.8 34.6 %copy-start.1 = (bf16[16,1,128,128]{3,2,1,0:T(8,128)(2,1)S(1)}, bf16[16,1,128,128]{3,2,1,0:T(8,128)(2,1)}, u32[]{:S(2)}) copy-start(bf16[16,1,128,128]{3,2,1,0:T(8,128)(2,1)} %param.8) | copy-start | bytes 1572868
  145.8 35.5 %copy-start.3 = (s32[16,1,32,1]{2,3,1,0:T(1,128)S(1)}, s32[16,1,32,1]{2,3,1,0:T(1,128)}, u32[]{:S(2)}) copy-start(s32[16,1,32,1]{2,3,1,0:T(1,128)} %param.7) | copy-start | bytes 6148
  150.0 3.2 copy-start
  156.2 72.3 %all-gather.33.cloned.1.call-start = ((), (), s32[]{:S(2)}) async-start(), calls=%async_computation.3 | async-start | bytes 2228224 | tf_op jit(solution)/shard_map/all_gather | solution.py:63
  181.3 110.7 %all-gather.35.cloned.1.call-start = ((), (), s32[]{:S(2)}) async-start(), calls=%async_computation.4 | async-start | bytes 1114112 | tf_op jit(solution)/shard_map/all_gather | solution.py:63
  235.3 121.0 %copy-start.2 = (bf16[16,1,128,128]{3,2,1,0:T(8,128)(2,1)S(1)}, bf16[16,1,128,128]{3,2,1,0:T(8,128)(2,1)}, u32[]{:S(2)}) copy-start(bf16[16,1,128,128]{3,2,1,0:T(8,128)(2,1)} %param.9) | copy-start | bytes 1572868
  249.9 103.7 %all-gather.37.cloned.1.call-start = ((), (), s32[]{:S(2)}) async-start(), calls=%async_computation.5 | async-start | bytes 1114112 | tf_op jit(solution)/shard_map/all_gather | solution.py:63
  311.6 89.1 %all-gather.39.cloned.1.call-start = ((), (), s32[]{:S(2)}) async-start(), calls=%async_computation.6 | async-start | bytes 1114112 | tf_op jit(solution)/shard_map/all_gather | solution.py:63
  358.0 107.4 %all-gather.41.cloned.1.call-start = ((), (), s32[]{:S(2)}) async-start(), calls=%async_computation.7 | async-start | bytes 1114112 | tf_op jit(solution)/shard_map/all_gather | solution.py:63
  423.3 69.8 %all-gather.43.cloned.1.call-start = ((), (), s32[]{:S(2)}) async-start(), calls=%async_computation.8 | async-start | bytes 1179648 | tf_op jit(solution)/shard_map/all_gather | solution.py:56
  470.5 72.3 %all-gather.45.cloned.1.call-start = ((), (), s32[]{:S(2)}) async-start(), calls=%async_computation.9 | async-start | bytes 2228224 | tf_op jit(solution)/shard_map/all_gather | solution.py:63
  495.6 80.8 %all-gather.47.cloned.1.call-start = ((), (), s32[]{:S(2)}) async-start(), calls=%async_computation.10 | async-start | bytes 2359296 | tf_op jit(solution)/shard_map/all_gather | solution.py:56
  551.7 85.4 %all-gather.49.cloned.1.call-start = ((), (), s32[]{:S(2)}) async-start(), calls=%async_computation.11 | async-start | bytes 4456448 | tf_op jit(solution)/shard_map/all_gather | solution.py:63
Sparse Core Ops, SparseCore 0:
  10.5 72.1 all-gather.26
  84.9 54.4 all-gather.28
  156.4 22.5 all-gather.30
  181.4 47.0 all-gather.32
  250.0 41.8 all-gather.34
  311.7 41.8 all-gather.36
  358.1 42.5 all-gather.38
  423.5 41.8 all-gather.40
  470.6 22.5 all-gather.42
  495.7 47.0 all-gather.44
  551.8 24.5 all-gather.46
  579.7 57.3 all-gather.48
